TPU v7x, 512 devices: a whole 4x8x8 slice. The times are simulated.
512 devices in a mesh: blk: 64 (over x, y, z_hi), uly: 8 (over z_lo, core).
Axes of the slice: x: 4, y: 8, z: 8 (z_hi: 2, z_lo: 4; z = z_hi * 4 + z_lo), core: 2. Of those that a mesh axis runs over, the one named last changes fastest.
Arguments:
- residual: bfloat16 [6144, 2048], P(('blk', 'uly')), may hold values from -24 to 24
- query_projection: bfloat16 [6144, 4096], P(('blk', 'uly')), may hold values from -51 to 51
- key_projection: bfloat16 [6144, 1024], P(('blk', 'uly')), may hold values from -5.1 to 5.1
- value_projection: bfloat16 [6144, 1024], P(('blk', 'uly')), may hold values from -6 to 6
- gate_proj: bfloat16 [6144, 4096], P(('blk', 'uly')), may hold values from -6 to 6
- positions: int32 [6144], replicated, may hold values from 0 to 6143, each once
- prefix_len: int32 [1], replicated, may hold values from 768 to 3071
- out_weight: bfloat16 [4096, 2048], P('uly', 'blk'), may hold values from -0.375 to 0.375
- norm_gain: float32 [2048], replicated, may hold values from 0.1 to 1.9
- gate_weight: bfloat16 [2048, 6144], P('blk', 'uly'), may hold values from -0.125 to 0.125
- up_weight: bfloat16 [2048, 6144], P('blk', 'uly'), may hold values from -0.125 to 0.125
- down_weight: bfloat16 [6144, 2048], P('uly', 'blk'), may hold values from -0.078125 to 0.078125
Outputs:
- layer_out: bfloat16 [6144, 2048], P(('blk', 'uly'))
Inputs may be any that keep to these rules, and one draw needn't show every extreme that they name: `positions`: each of 0 to 6143 appears once.
All inputs are finite; a program needn't handle non-finite values.
Results may differ from a plain program's by a relative error of at most 0.014.
Values may be sent and summed in bfloat16 or wider, within the bound.
A program may use at most 64 MiB of HBM per device.

v0:
```python
import math
import jax
import jax.numpy as jnp
from jax import lax
from jax.sharding import PartitionSpec as P

HEAD_SIZE = 128


def per_device(
    residual,
    query_projection,
    key_projection,
    value_projection,
    gate_proj,
    positions,
    prefix_len,
    out_weight,
    norm_gain,
    gate_weight,
    up_weight,
    down_weight,
):
    q_loc, k_loc, v_loc, g_loc = (
        lax.all_to_all(query_projection, "uly", split_axis=1, concat_axis=0, tiled=True),
        lax.all_to_all(key_projection, "uly", split_axis=1, concat_axis=0, tiled=True),
        lax.all_to_all(value_projection, "uly", split_axis=1, concat_axis=0, tiled=True),
        lax.all_to_all(gate_proj, "uly", split_axis=1, concat_axis=0, tiled=True),
    )
    row_count = q_loc.shape[0]
    kv_heads = k_loc.shape[1] // HEAD_SIZE
    q_heads = q_loc.shape[1] // HEAD_SIZE
    heads_per_group = q_heads // kv_heads
    score_scale = 1.0 / math.sqrt(HEAD_SIZE)
    blk_index = lax.axis_index("blk")
    query_pos = lax.dynamic_slice_in_dim(positions, blk_index * row_count, row_count)
    prefix = prefix_len[0]
    query_heads = q_loc.reshape(row_count, kv_heads, heads_per_group, HEAD_SIZE)
    wo_full, wg_full, wu_full, wd_full = (
        lax.all_gather(out_weight, "blk", axis=1, tiled=True),
        lax.all_gather(gate_weight, "blk", axis=0, tiled=True),
        lax.all_gather(up_weight, "blk", axis=0, tiled=True),
        lax.all_gather(down_weight, "blk", axis=1, tiled=True),
    )
    run_max = jnp.full((row_count, kv_heads, heads_per_group), -jnp.inf, jnp.float32)
    run_sum = jnp.zeros((row_count, kv_heads, heads_per_group), jnp.float32)
    weighted = jnp.zeros((row_count, kv_heads, heads_per_group, HEAD_SIZE), jnp.float32)
    key_part = lax.all_gather(k_loc, "blk", axis=0, tiled=True)
    value_part = lax.all_gather(v_loc, "blk", axis=0, tiled=True)
    key_count = key_part.shape[0]
    scores = (
        jnp.einsum(
            "bkgd,skd->bkgs",
            query_heads,
            key_part.reshape(key_count, kv_heads, HEAD_SIZE),
            preferred_element_type=jnp.float32,
        )
        * score_scale
    )
    visible = (positions[None, :] <= query_pos[:, None]) | (positions[None, :] < prefix)
    scores = jnp.where(visible[:, None, None, :], scores, -jnp.inf)
    new_max = jnp.max(scores, axis=-1)
    safe_max = jnp.where(new_max == -jnp.inf, 0.0, new_max)
    factor = jnp.exp(run_max - safe_max)
    exp_scores = jnp.exp(scores - safe_max[..., None])
    run_sum = run_sum * factor + jnp.sum(exp_scores, axis=-1)
    probs = exp_scores.astype(jnp.bfloat16)
    weighted = weighted * factor[..., None] + jnp.einsum(
        "bkgs,skd->bkgd",
        probs,
        value_part.reshape(key_count, kv_heads, HEAD_SIZE),
        preferred_element_type=jnp.float32,
    )
    _, denom, weighted = (new_max, run_sum, weighted)
    attended = (weighted / denom[..., None]).reshape(row_count, q_heads * HEAD_SIZE)
    gated_out = (attended * jax.nn.sigmoid(g_loc.astype(jnp.float32))).astype(jnp.bfloat16)
    head_partial = jnp.dot(gated_out, wo_full, preferred_element_type=jnp.float32)
    projected = lax.psum_scatter(
        head_partial.astype(jnp.bfloat16), "uly", scatter_dimension=0, tiled=True
    ).astype(jnp.float32)
    hidden_f = (residual.astype(jnp.float32) + projected).astype(jnp.bfloat16).astype(jnp.float32)
    mean_sq = jnp.mean(hidden_f * hidden_f, axis=-1, keepdims=True)
    normed = (hidden_f * lax.rsqrt(mean_sq + 1e-06) * norm_gain).astype(jnp.bfloat16)
    group_rows = lax.all_gather(normed, "uly", axis=0, tiled=True)
    gate_sum = jnp.dot(group_rows, wg_full, preferred_element_type=jnp.float32)
    up_sum = jnp.dot(group_rows, wu_full, preferred_element_type=jnp.float32)
    activated = (jax.nn.silu(gate_sum) * up_sum).astype(jnp.bfloat16)
    ffn_partial = jnp.dot(activated, wd_full, preferred_element_type=jnp.float32)
    ffn_out = lax.psum_scatter(
        ffn_partial.astype(jnp.bfloat16), "uly", scatter_dimension=0, tiled=True
    ).astype(jnp.float32)
    return (hidden_f + ffn_out).astype(jnp.bfloat16)


def solution(mesh):
    return jax.shard_map(
        per_device,
        mesh=mesh,
        in_specs=(
            P(("blk", "uly"), None),
            P(("blk", "uly"), None),
            P(("blk", "uly"), None),
            P(("blk", "uly"), None),
            P(("blk", "uly"), None),
            P(),
            P(),
            P("uly", "blk"),
            P(),
            P("blk", "uly"),
            P("blk", "uly"),
            P("uly", "blk"),
        ),
        out_specs=P(("blk", "uly"), None),
        check_vma=False,
    )
```

profile of v0, /device:TPU:1, one launch (start us, length us, event | category | flops | bytes accessed | tf_op | source)
XLA Modules:
  0.0 897.3 jit_solution(13046254227862782462)
XLA Ops:
  6.5 0.8 copy.27
  7.3 14.2 %all_to_all.67 = bf16[12,8,128]{2,0,1:T(8,128)(2,1)S(1)} all-to-all(bf16[12,8,128]{2,0,1:T(8,128)(2,1)S(1)} %copy.21), channel_id=1, replica_groups=mesh['blk'=64,'uly'=8] {'uly'}, dimensions={1} | all-to-all | bytes 49152 | tf_op jit(solution)/shard_map/all_to_all | solution.py:26
  21.5 0.6 all_to_all.53
  22.1 0.0 all-gather.8.cloned.1.call-update
  22.1 0.0 all-gather.10.cloned.1.call-start
  22.2 0.8 copy.29
  23.0 8.1 all_to_all.68
  31.1 0.6 all_to_all.60
  31.7 0.0 all-gather.10.cloned.1.call-update
  31.7 0.0 all-gather.12.cloned.1.call-start
  31.8 0.7 all-gather.12.cloned.1.call-update
  32.5 0.0 all-gather.14.cloned.1.call-start
  32.5 0.5 all-gather.14.cloned.1.call-update
  33.0 0.0 all-gather.16.cloned.1.call-start
  33.1 0.5 all-gather.16.cloned.1.call-update
  33.6 0.9 copy.28
  34.6 0.7 copy.22
  35.3 4.0 all-to-all-start.1
  39.3 0.0 all-gather.18.cloned.1.call-start
  39.3 0.6 all-gather.18.cloned.1.call-update
  40.5 0.9 copy.31
  41.5 0.7 copy.26
  42.2 0.8 dynamic_slice.3
  43.0 0.7 broadcast_compare_fusion
  43.7 1.5 all-to-all-done.1
  45.2 4.3 all-to-all-start.3
  49.6 1.2 compare_or_fusion
  50.8 4.6 all-to-all-done.3
  55.4 0.1 divide_bitcast_fusion
  55.5 97.2 %all-gather.8.cloned.1.call-done = bf16[6144,128]{1,0:T(8,128)(2,1)} async-done(((bf16[96,128]{1,0:T(8,128)(2,1)}), bf16[6144,128]{1,0:T(8,128)(2,1)}) %all-gather.8.cloned.1.call-update) | async-done | bytes 1572880 | tf_op jit(solution)/shard_map/all_gather | solution.py:48
  152.7 3.3 fusion.47
  156.0 1.4 fusion.2
  157.4 2.2 copy-done
  159.7 124.8 %all-gather.10.cloned.1.call-done = bf16[6144,128]{1,0:T(8,128)(2,1)} async-done(((bf16[96,128]{1,0:T(8,128)(2,1)}), bf16[6144,128]{1,0:T(8,128)(2,1)}) %all-gather.10.cloned.1.call-update) | async-done | bytes 1572880 | tf_op jit(solution)/shard_map/all_gather | solution.py:49
  284.4 5.6 fusion.26
  290.0 0.0 copy-start.1
  290.0 0.0 copy-start.2
  290.0 0.1 copy.25
  290.1 131.4 %all-gather.12.cloned.1.call-done = bf16[512,2048]{0,1:T(8,128)(2,1)} async-done(((bf16[512,32]{0,1:T(8,128)(2,1)}), bf16[512,2048]{0,1:T(8,128)(2,1)}) %all-gather.12.cloned.1.call-update) | async-done | bytes 2097168 | tf_op jit(solution)/shard_map/all_gather | solution.py:40
  421.6 2.3 convolution_convert_fusion
  423.9 21.0 %fusion = bf16[16,2048]{1,0:T(8,128)(2,1)S(1)} fusion(bf16[96,2048]{1,0:T(8,128)(2,1)S(1)} %convolution_convert_fusion), kind=kCustom, calls=%all-reduce-scatter | all-reduce-scatter fusion | flops 262145 | bytes 460800
  445.0 1.9 collective-permute-start
  446.9 2.2 collective-permute-start.1
  449.1 1.3 dynamic-slice.6
  451.1 0.0 collective-permute-done.1
  451.1 0.0 collective-permute-done
  451.1 0.4 concatenate
  451.5 0.2 fusion.38
  451.7 0.0 copy-done.2
  451.7 0.1 fusion.44
  451.8 15.2 %all-gather = bf16[8,12,2048]{2,1,0:T(8,128)(2,1)S(1)} all-gather(bf16[1,12,2048]{2,1,0:T(8,128)(2,1)S(1)} %fusion.44), channel_id=1, replica_groups=mesh['blk'=64,'uly'=8] {'uly'}, dimensions={0}, use_global_device_ids=true | all-gather | bytes 442368 | tf_op jit(solution)/shard_map/all_gather | solution.py:84
  467.0 0.1 reshape.132
  467.1 100.4 %all-gather.14.cloned.1.call-done = bf16[2048,768]{1,0:T(8,128)(2,1)} async-done(((bf16[32,768]{1,0:T(8,128)(2,1)}), bf16[2048,768]{1,0:T(8,128)(2,1)}) %all-gather.14.cloned.1.call-update) | async-done | bytes 3145744 | tf_op jit(solution)/shard_map/all_gather | solution.py:41
  567.5 2.5 fusion.48
  570.0 143.2 %all-gather.16.cloned.1.call-done = bf16[2048,768]{1,0:T(8,128)(2,1)} async-done(((bf16[32,768]{1,0:T(8,128)(2,1)}), bf16[2048,768]{1,0:T(8,128)(2,1)}) %all-gather.16.cloned.1.call-update) | async-done | bytes 3145744 | tf_op jit(solution)/shard_map/all_gather | solution.py:42
  713.3 145.8 %all-gather.18.cloned.1.call-done = bf16[768,2048]{0,1:T(8,128)(2,1)} async-done(((bf16[768,32]{0,1:T(8,128)(2,1)}), bf16[768,2048]{0,1:T(8,128)(2,1)}) %all-gather.18.cloned.1.call-update) | async-done | bytes 3145744 | tf_op jit(solution)/shard_map/all_gather | solution.py:43
  859.0 4.6 convolution_convert_fusion.1
  863.6 20.3 %fusion.1 = bf16[16,2048]{1,0:T(8,128)(2,1)S(1)} fusion(bf16[96,2048]{1,0:T(8,128)(2,1)S(1)} %convolution_convert_fusion.1), kind=kCustom, calls=%all-reduce-scatter.1 | all-reduce-scatter fusion | flops 262145 | bytes 460800
  883.9 1.9 collective-permute-start.2
  885.8 2.3 collective-permute-start.3
  888.1 1.3 collective-permute-done.3
  889.4 0.0 collective-permute-done.2
  889.4 0.4 concatenate.1
  889.8 0.7 fusion.41
  (16 shorter events, 0.2 us)
Async XLA Ops:
  6.5 146.1 %all-gather.8.cloned.1.call-start = ((), (), s32[]{:S(2)}) async-start(), calls=%async_computation.4 | async-start | bytes 1597440 | tf_op jit(solution)/shard_map/all_gather | solution.py:48
  22.1 262.3 %all-gather.10.cloned.1.call-start = ((), (), s32[]{:S(2)}) async-start(), calls=%async_computation.5 | async-start | bytes 1597440 | tf_op jit(solution)/shard_map/all_gather | solution.py:49
  31.7 389.9 %all-gather.12.cloned.1.call-start = ((), (), s32[]{:S(2)}) async-start(), calls=%async_computation.6 | async-start | bytes 2129920 | tf_op jit(solution)/shard_map/all_gather | solution.py:40
  32.5 535.0 %all-gather.14.cloned.1.call-start = ((), (), s32[]{:S(2)}) async-start(), calls=%async_computation.7 | async-start | bytes 3194880 | tf_op jit(solution)/shard_map/all_gather | solution.py:41
  33.0 680.2 %all-gather.16.cloned.1.call-start = ((), (), s32[]{:S(2)}) async-start(), calls=%async_computation.8 | async-start | bytes 3194880 | tf_op jit(solution)/shard_map/all_gather | solution.py:42
  35.3 10.0 %all-to-all-start.1 = ((bf16[12,8,512]{2,0,1:T(8,128)(2,1)}), bf16[12,8,512]{2,0,1:T(8,128)(2,1)S(1)}, u32[]{:S(2)}, u32[]{:S(2)}) async-start(bf16[12,8,512]{2,0,1:T(8,128)(2,1)} %copy.22), calls=%async_computation.1 | async-start | bytes 262144 | tf_op jit(solution)/shard_map/all_to_all | solution.py:25
  39.3 819.7 %all-gather.18.cloned.1.call-start = ((), (), s32[]{:S(2)}) async-start(), calls=%async_computation.9 | async-start | bytes 3194880 | tf_op jit(solution)/shard_map/all_gather | solution.py:43
  45.2 10.2 %all-to-all-start.3 = ((bf16[12,8,512]{2,0,1:T(8,128)(2,1)}), bf16[12,8,512]{2,0,1:T(8,128)(2,1)S(1)}, u32[]{:S(2)}, u32[]{:S(2)}) async-start(bf16[12,8,512]{2,0,1:T(8,128)(2,1)} %copy.26), calls=%async_computation.3 | async-start | bytes 262144 | tf_op jit(solution)/shard_map/all_to_all | solution.py:28
  156.0 3.7 copy-start
  290.0 161.5 %copy-start.1 = (bf16[12,2048]{1,0:T(8,128)(2,1)S(1)}, bf16[12,2048]{1,0:T(8,128)(2,1)}, u32[]{:S(2)}) copy-start(bf16[12,2048]{1,0:T(8,128)(2,1)} %param.12) | copy-start | bytes 147460
  290.0 161.7 %copy-start.2 = (f32[2048]{0:T(1024)S(1)}, f32[2048]{0:T(1024)}, u32[]{:S(2)}) copy-start(f32[2048]{0:T(1024)} %param.20) | copy-start | bytes 24580
  445.0 6.1 collective-permute-start
  446.9 4.1 collective-permute-start.1
  883.9 5.5 collective-permute-start.2
  885.8 3.6 collective-permute-start.3
Sparse Core Ops, SparseCore 0:
  22.3 130.3 all-gather.7
  157.1 127.2 all-gather.9
  288.9 132.6 all-gather.11
  425.9 141.5 all-gather.13
  571.8 141.4 all-gather.15
  717.6 141.4 all-gather.17
where the time goes:
time: 898 us; the launch traced here: 897 us
  waiting for transfers between devices  753 us (84%)
  blocking collectives  78.8 us (9%)
  matrix products  18.3 us (2%)
  starting transfers between devices  16.9 us (2%)
  between operations  15 us (2%)
  local copies, waits for them, and re-layouts  11.4 us (1%)
    all_gather x1, waiting for transfers between devices, per_device(): lax.all_gather(down_weight, 'blk', axis=1, tiled=True)  146 us
    all_gather x1, waiting for transfers between devices, per_device(): lax.all_gather(up_weight, 'blk', axis=0, tiled=True)  143 us
    all_gather x1, waiting for transfers between devices, per_device(): lax.all_gather(out_weight, 'blk', axis=1, tiled=True)  131 us
    all_gather x1, waiting for transfers between devices, per_device(): value_part = lax.all_gather(v_loc, 'blk', axis=0, tiled=True)  125 us
    all_gather x1, waiting for transfers between devices, per_device(): lax.all_gather(gate_weight, 'blk', axis=0, tiled=True)  100 us
    all_gather x1, waiting for transfers between devices, per_device(): key_part = lax.all_gather(k_loc, 'blk', axis=0, tiled=True)  97.2 us
    unnamed x2, blocking collectives  41.3 us
  transfers between devices with their start and end apart: 12, of which 9 were waited for; matrix products, arithmetic and copies ran while one was open for 5% of the time, Pallas kernels for 0%

commit v1 on v0

--- a/solution.py
+++ b/solution.py
@@ -45,7 +45,12 @@
     run_max = jnp.full((row_count, kv_heads, heads_per_group), -jnp.inf, jnp.float32)
     run_sum = jnp.zeros((row_count, kv_heads, heads_per_group), jnp.float32)
     weighted = jnp.zeros((row_count, kv_heads, heads_per_group, HEAD_SIZE), jnp.float32)
-    key_part = lax.all_gather(k_loc, "blk", axis=0, tiled=True)
+    key_part = jnp.concatenate(
+        lax.all_to_all(
+            jnp.stack(lax.axis_size("blk") * [k_loc]), axis_name="blk", split_axis=0, concat_axis=0
+        ),
+        axis=0,
+    )
     value_part = lax.all_gather(v_loc, "blk", axis=0, tiled=True)
     key_count = key_part.shape[0]
     scores = (

time: 898 us -> 790 us (0.88)
  waiting for transfers between devices: 753 us -> 636 us
  starting transfers between devices: 16.9 us -> 36.2 us
    all_gather x1 -> x0, waiting for transfers between devices: 97.2 us -> none  [per_device(): key_part = lax.all_gather(k_loc, 'blk', axis=0, tiled=True)]
    all_gather x1, waiting for transfers between devices: 125 us -> 56.8 us  [per_device(): value_part = lax.all_gather(v_loc, 'blk', axis=0, tiled=True)]
    all_to_all x0 -> x2, waiting for transfers between devices: none -> 44 us  [the longest x1 40.7 us: per_device(): lax.all_to_all(jnp.stack(lax.axis_size('blk') * [k_loc]), axis_name='blk'...]
    all_to_all x0 -> x2, starting transfers between devices: none -> 19.3 us  [the longest x1 15.3 us: per_device(): lax.all_to_all(jnp.stack(lax.axis_size('blk') * [k_loc]), axis_name='blk'...]
    all_to_all x1 -> x0, blocking collectives: 14.2 us -> none  [per_device(): lax.all_to_all(key_projection, 'uly', split_axis=1, concat_axis=0, tiled=...]
  transfers between devices with their start and end apart: 12 -> 13, of which waited for: 9 -> 10; matrix products, arithmetic and copies ran while one was open for 5% -> 6% of each run, Pallas kernels for 0% -> 0%
where the time goes in v1:
time: 790 us; the launch traced here: 789 us
  waiting for transfers between devices  636 us (81%)
  blocking collectives  70.8 us (9%)
  starting transfers between devices  36.2 us (5%)
  matrix products  16.8 us (2%)
  between operations  14.7 us (2%)
  local copies, waits for them, and re-layouts  12.1 us (2%)
    all_gather x1, waiting for transfers between devices, per_device(): lax.all_gather(down_weight, 'blk', axis=1, tiled=True)  146 us
    all_gather x1, waiting for transfers between devices, per_device(): lax.all_gather(up_weight, 'blk', axis=0, tiled=True)  143 us
    all_gather x1, waiting for transfers between devices, per_device(): lax.all_gather(out_weight, 'blk', axis=1, tiled=True)  131 us
    all_gather x1, waiting for transfers between devices, per_device(): lax.all_gather(gate_weight, 'blk', axis=0, tiled=True)  100 us
    all_gather x1, waiting for transfers between devices, per_device(): value_part = lax.all_gather(v_loc, 'blk', axis=0, tiled=True)  56.8 us
    unnamed x2, blocking collectives  41.3 us
    all_to_all x1, waiting for transfers between devices, per_device(): lax.all_to_all(jnp.stack(lax.axis_size('blk') * [k_loc]), axis_name='blk'...  40.7 us
  transfers between devices with their start and end apart: 13, of which 10 were waited for; matrix products, arithmetic and copies ran while one was open for 6% of the time, Pallas kernels for 0%

profile of v1, /device:TPU:1, one launch (start us, length us, event | category | flops | bytes accessed | tf_op | source)
XLA Modules:
  0.0 789.0 jit_solution(9402865728141464766)
XLA Ops:
  6.5 0.8 copy.28
  7.3 14.2 %all_to_all.69 = bf16[12,8,128]{2,0,1:T(8,128)(2,1)S(1)} all-to-all(bf16[12,8,128]{2,0,1:T(8,128)(2,1)S(1)} %copy.23), channel_id=1, replica_groups=mesh['blk'=64,'uly'=8] {'uly'}, dimensions={1} | all-to-all | bytes 49152 | tf_op jit(solution)/shard_map/all_to_all | solution.py:27
  21.5 0.6 all_to_all.61
  22.1 0.0 all-gather.7.cloned.1.call-update
  22.1 0.0 all-gather.9.cloned.1.call-start
  22.2 0.7 all-gather.9.cloned.1.call-update
  22.9 0.0 all-gather.11.cloned.1.call-start
  22.9 0.7 all-gather.11.cloned.1.call-update
  23.6 0.0 all-gather.13.cloned.1.call-start
  23.7 0.5 all-gather.13.cloned.1.call-update
  24.2 0.8 copy.26
  25.0 0.6 copy.20
  25.6 4.0 all-to-all-start
  29.6 0.9 copy.27
  30.6 0.0 copy-start.1
  30.6 0.7 copy.21
  31.3 3.3 all-to-all-done
  34.6 4.0 all-to-all-start.2
  38.7 0.9 copy.30
  39.6 0.7 copy.25
  40.3 4.2 all-to-all-done.2
  44.5 4.3 all-to-all-start.4
  48.8 5.8 all-to-all-done.4
  54.6 1.4 stack.5
  56.0 15.3 %all-to-all-start.1 = ((bf16[64,96,128]{2,1,0:T(8,128)(2,1)}), bf16[64,96,128]{2,1,0:T(8,128)(2,1)S(1)}, u32[]{:S(2)}, u32[]{:S(2)}) async-start(bf16[64,96,128]{2,1,0:T(8,128)(2,1)} %stack.5), calls=%async_computation.1 | async-start | bytes 3145728 | tf_op jit(solution)/shard_map/all_to_all | solution.py:49
  71.3 0.0 all-gather.15.cloned.1.call-start
  71.4 0.5 all-gather.15.cloned.1.call-update
  72.6 0.1 dynamic_slice.3
  72.7 0.5 compare_or_fusion
  73.2 0.1 divide_bitcast_fusion
  73.3 40.7 %all-to-all-done.1 = bf16[64,96,128]{2,1,0:T(8,128)(2,1)S(1)} async-done(((bf16[64,96,128]{2,1,0:T(8,128)(2,1)}), bf16[64,96,128]{2,1,0:T(8,128)(2,1)S(1)}, u32[]{:S(2)}, u32[]{:S(2)}) %all-to-all-start.1) | async-done | bytes 1572896 | tf_op jit(solution)/shard_map/all_to_all | solution.py:49
  114.0 1.8 fusion.46
  115.8 1.4 fusion.2
  117.3 2.2 copy-done
  119.5 56.8 %all-gather.7.cloned.1.call-done = bf16[6144,128]{1,0:T(8,128)(2,1)} async-done(((bf16[96,128]{1,0:T(8,128)(2,1)}), bf16[6144,128]{1,0:T(8,128)(2,1)}) %all-gather.7.cloned.1.call-update) | async-done | bytes 1572880 | tf_op jit(solution)/shard_map/all_gather | solution.py:54
  176.3 5.6 fusion.25
  181.9 0.0 copy-start.2
  181.9 0.0 copy-start.3
  181.9 0.1 copy.24
  182.1 131.4 %all-gather.9.cloned.1.call-done = bf16[512,2048]{0,1:T(8,128)(2,1)} async-done(((bf16[512,32]{0,1:T(8,128)(2,1)}), bf16[512,2048]{0,1:T(8,128)(2,1)}) %all-gather.9.cloned.1.call-update) | async-done | bytes 2097168 | tf_op jit(solution)/shard_map/all_gather | solution.py:40
  313.5 2.4 convolution_convert_fusion
  315.9 21.0 %fusion = bf16[16,2048]{1,0:T(8,128)(2,1)S(1)} fusion(bf16[96,2048]{1,0:T(8,128)(2,1)S(1)} %convolution_convert_fusion), kind=kCustom, calls=%all-reduce-scatter | all-reduce-scatter fusion | flops 262145 | bytes 460800
  336.9 1.9 collective-permute-start
  338.8 2.2 collective-permute-start.1
  341.0 1.3 dynamic-slice.6
  343.0 0.0 collective-permute-done.1
  343.0 0.0 collective-permute-done
  343.0 0.4 concatenate
  343.4 0.2 fusion.37
  343.6 0.1 fusion.43
  343.7 15.3 %all-gather = bf16[8,12,2048]{2,1,0:T(8,128)(2,1)S(1)} all-gather(bf16[1,12,2048]{2,1,0:T(8,128)(2,1)S(1)} %fusion.43), channel_id=1, replica_groups=mesh['blk'=64,'uly'=8] {'uly'}, dimensions={0}, use_global_device_ids=true | all-gather | bytes 442368 | tf_op jit(solution)/shard_map/all_gather | solution.py:89
  359.0 0.1 reshape.137
  359.0 100.5 %all-gather.11.cloned.1.call-done = bf16[2048,768]{1,0:T(8,128)(2,1)} async-done(((bf16[32,768]{1,0:T(8,128)(2,1)}), bf16[2048,768]{1,0:T(8,128)(2,1)}) %all-gather.11.cloned.1.call-update) | async-done | bytes 3145744 | tf_op jit(solution)/shard_map/all_gather | solution.py:41
  459.5 2.5 fusion.47
  462.1 143.3 %all-gather.13.cloned.1.call-done = bf16[2048,768]{1,0:T(8,128)(2,1)} async-done(((bf16[32,768]{1,0:T(8,128)(2,1)}), bf16[2048,768]{1,0:T(8,128)(2,1)}) %all-gather.13.cloned.1.call-update) | async-done | bytes 3145744 | tf_op jit(solution)/shard_map/all_gather | solution.py:42
  605.3 145.8 %all-gather.15.cloned.1.call-done = bf16[768,2048]{0,1:T(8,128)(2,1)} async-done(((bf16[768,32]{0,1:T(8,128)(2,1)}), bf16[768,2048]{0,1:T(8,128)(2,1)}) %all-gather.15.cloned.1.call-update) | async-done | bytes 3145744 | tf_op jit(solution)/shard_map/all_gather | solution.py:43
  751.1 4.5 convolution_convert_fusion.1
  755.6 20.3 %fusion.1 = bf16[16,2048]{1,0:T(8,128)(2,1)S(1)} fusion(bf16[96,2048]{1,0:T(8,128)(2,1)S(1)} %convolution_convert_fusion.1), kind=kCustom, calls=%all-reduce-scatter.1 | all-reduce-scatter fusion | flops 262145 | bytes 460800
  775.9 1.9 collective-permute-start.2
  777.9 2.3 collective-permute-start.3
  780.1 1.3 collective-permute-done.3
  781.4 0.0 collective-permute-done.2
  781.4 0.4 concatenate.1
  781.8 0.7 fusion.40
  (19 shorter events, 0.2 us)
Async XLA Ops:
  6.5 169.8 %all-gather.7.cloned.1.call-start = ((), (), s32[]{:S(2)}) async-start(), calls=%async_computation.5 | async-start | bytes 1597440 | tf_op jit(solution)/shard_map/all_gather | solution.py:54
  22.1 291.4 %all-gather.9.cloned.1.call-start = ((), (), s32[]{:S(2)}) async-start(), calls=%async_computation.6 | async-start | bytes 2129920 | tf_op jit(solution)/shard_map/all_gather | solution.py:40
  22.9 436.7 %all-gather.11.cloned.1.call-start = ((), (), s32[]{:S(2)}) async-start(), calls=%async_computation.7 | async-start | bytes 3194880 | tf_op jit(solution)/shard_map/all_gather | solution.py:41
  23.6 581.7 %all-gather.13.cloned.1.call-start = ((), (), s32[]{:S(2)}) async-start(), calls=%async_computation.8 | async-start | bytes 3194880 | tf_op jit(solution)/shard_map/all_gather | solution.py:42
  25.6 9.0 %all-to-all-start = ((bf16[12,8,128]{2,0,1:T(8,128)(2,1)}), bf16[12,8,128]{2,0,1:T(8,128)(2,1)S(1)}, u32[]{:S(2)}, u32[]{:S(2)}) async-start(bf16[12,8,128]{2,0,1:T(8,128)(2,1)} %copy.20), calls=%async_computation | async-start | bytes 65536 | tf_op jit(solution)/shard_map/all_to_all | solution.py:26
  30.6 42.0 %copy-start.1 = (s32[6144]{0:T(1024)S(1)}, s32[6144]{0:T(1024)}, u32[]{:S(2)}) copy-start(s32[6144]{0:T(1024)} %param.17) | copy-start | bytes 73732
  34.6 9.9 %all-to-all-start.2 = ((bf16[12,8,512]{2,0,1:T(8,128)(2,1)}), bf16[12,8,512]{2,0,1:T(8,128)(2,1)S(1)}, u32[]{:S(2)}, u32[]{:S(2)}) async-start(bf16[12,8,512]{2,0,1:T(8,128)(2,1)} %copy.21), calls=%async_computation.2 | async-start | bytes 262144 | tf_op jit(solution)/shard_map/all_to_all | solution.py:25
  44.5 10.1 %all-to-all-start.4 = ((bf16[12,8,512]{2,0,1:T(8,128)(2,1)}), bf16[12,8,512]{2,0,1:T(8,128)(2,1)S(1)}, u32[]{:S(2)}, u32[]{:S(2)}) async-start(bf16[12,8,512]{2,0,1:T(8,128)(2,1)} %copy.25), calls=%async_computation.4 | async-start | bytes 262144 | tf_op jit(solution)/shard_map/all_to_all | solution.py:28
  56.0 58.0 %all-to-all-start.1 = ((bf16[64,96,128]{2,1,0:T(8,128)(2,1)}), bf16[64,96,128]{2,1,0:T(8,128)(2,1)S(1)}, u32[]{:S(2)}, u32[]{:S(2)}) async-start(bf16[64,96,128]{2,1,0:T(8,128)(2,1)} %stack.5), calls=%async_computation.1 | async-start | bytes 3145728 | tf_op jit(solution)/shard_map/all_to_all | solution.py:49
  71.3 679.7 %all-gather.15.cloned.1.call-start = ((), (), s32[]{:S(2)}) async-start(), calls=%async_computation.9 | async-start | bytes 3194880 | tf_op jit(solution)/shard_map/all_gather | solution.py:43
  115.8 3.7 copy-start
  181.9 161.5 %copy-start.2 = (bf16[12,2048]{1,0:T(8,128)(2,1)S(1)}, bf16[12,2048]{1,0:T(8,128)(2,1)}, u32[]{:S(2)}) copy-start(bf16[12,2048]{1,0:T(8,128)(2,1)} %param.12) | copy-start | bytes 147460
  181.9 161.6 %copy-start.3 = (f32[2048]{0:T(1024)S(1)}, f32[2048]{0:T(1024)}, u32[]{:S(2)}) copy-start(f32[2048]{0:T(1024)} %param.20) | copy-start | bytes 24580
  336.9 6.1 collective-permute-start
  338.8 4.1 collective-permute-start.1
  775.9 5.5 collective-permute-start.2
  777.9 3.6 collective-permute-start.3
Sparse Core Ops, SparseCore 0:
  22.3 154.0 all-gather.6
  180.8 132.6 all-gather.8
  317.9 141.5 all-gather.10
  463.8 141.4 all-gather.12
  609.6 141.4 all-gather.14
